TPU v7x, 128 devices: a whole 4x4x4 slice. The times are simulated.
128 devices in a mesh: feed: 32 (over y_hi, x, z), tm: 4 (over y_lo, core).
Axes of the slice: x: 4, y: 4 (y_hi: 2, y_lo: 2; y = y_hi * 2 + y_lo), z: 4, core: 2. Of those that a mesh axis runs over, the one named last changes fastest.
Arguments:
- voltages: int32 [512, 524288], P('feed', 'tm'), may hold values from -128 to 127, as said below
- pfb_taps: float32 [16, 2048], replicated, may hold values from -3 to 3
- feed_flags: int32 [512], P('feed'), may hold values 0 or 1
Outputs:
- visibility: float32 [1024, 2, 512, 512], P(('feed', 'tm'))
Inputs may be any that keep to these rules, and one draw needn't show every extreme that they name: `voltages`: signed 8-bit sample values.
All inputs are finite; a program needn't handle non-finite values. No bound on the sum of `feed_flags` on one device may be relied on, other than what follows from the above.
Results may differ from a plain program's by a relative error of at most 0.0019.
Values may be sent and summed in bfloat16 or wider, within the bound.
A program may use at most 128 MiB of HBM per device.

v0:
```python
import math

import jax
import jax.numpy as jnp
from jax import lax
from jax.sharding import PartitionSpec as P


def shifted(block, axis, distance):
    devices = range(lax.axis_size(axis))
    route = [(i - distance, i) for i in devices if i - distance in devices]
    return lax.ppermute(block, axis, route)


def dft_tables(frame_len, channels):
    row_index = lax.broadcasted_iota(jnp.int32, (channels, frame_len), 0)
    sample_index = lax.broadcasted_iota(jnp.int32, (channels, frame_len), 1)
    phase_step = row_index * sample_index % frame_len
    phase_angle = phase_step.astype(jnp.float32) * (2.0 * math.pi / frame_len)
    dft_table = jnp.concatenate([jnp.cos(phase_angle), -jnp.sin(phase_angle)], axis=0)
    table_high = dft_table.astype(jnp.bfloat16)
    table_low = (dft_table - table_high.astype(jnp.float32)).astype(jnp.bfloat16)
    return (table_high, table_low)


def batched_gram(left_part, right_part):
    numbers = (((2,), (2,)), ((0,), (0,)))
    return lax.dot_general(left_part, right_part, numbers, preferred_element_type=jnp.float32)


def cross_pair(real_rows, imag_rows, real_cols, imag_cols):
    vis_real = batched_gram(real_rows, real_cols) + batched_gram(imag_rows, imag_cols)
    vis_imag = batched_gram(imag_rows, real_cols) - batched_gram(real_rows, imag_cols)
    return (vis_real, vis_imag)


def per_device(voltages, pfb_taps, feed_flags):
    inputs_dev = voltages.shape[0]
    taps_count = pfb_taps.shape[0]
    frame_len = pfb_taps.shape[1]
    spec_dev = voltages.shape[1] // frame_len
    channels = frame_len // 2
    feed_count = lax.axis_size("feed")
    time_count = lax.axis_size("tm")
    chan_dev = channels // (feed_count * time_count)
    all_inputs = feed_count * inputs_dev
    spectra_total = spec_dev * time_count
    samples = voltages.astype(jnp.bfloat16).reshape(inputs_dev, spec_dev, frame_len)
    rim_frames = samples[:, spec_dev - taps_count + 1 :, :]
    before = shifted(rim_frames, "tm", 1)
    frames = jnp.concatenate([before, samples], axis=1).astype(jnp.float32) / 128.0
    running = jnp.zeros((inputs_dev, spec_dev, frame_len), jnp.float32)
    for tap_lag in range(taps_count):
        offset = taps_count - 1 - tap_lag
        running = running + pfb_taps[tap_lag] * frames[:, offset : offset + spec_dev, :]
    kept_mask = feed_flags.astype(jnp.float32)[:, None, None]
    filtered = (running * kept_mask).astype(jnp.bfloat16).reshape(inputs_dev * spec_dev, frame_len)
    table_high, table_low = dft_tables(frame_len, channels)
    contract = (((1,), (1,)), ((), ()))
    transformed = lax.dot_general(
        table_high, filtered, contract, preferred_element_type=jnp.float32
    )
    transformed = transformed + lax.dot_general(
        table_low, filtered, contract, preferred_element_type=jnp.float32
    )
    spectra = (
        (transformed / math.sqrt(frame_len))
        .astype(jnp.bfloat16)
        .reshape(2, channels, inputs_dev, spec_dev)
    )
    turned = lax.all_to_all(spectra, ("feed", "tm"), split_axis=1, concat_axis=2, tiled=True)
    turned = turned.reshape(2, chan_dev, feed_count, time_count, inputs_dev, spec_dev)
    turned = jnp.transpose(turned, (0, 1, 2, 4, 3, 5)).reshape(
        2, chan_dev, all_inputs, spectra_total
    )
    real_all = turned[0]
    imag_all = turned[1]
    vis_real, vis_imag = cross_pair(real_all, imag_all, real_all, imag_all)
    return jnp.stack([vis_real, vis_imag], axis=1) / spectra_total


def solution(mesh):
    return jax.shard_map(
        per_device,
        mesh=mesh,
        in_specs=(P("feed", "tm"), P(), P("feed")),
        out_specs=P(("feed", "tm"), None, None, None),
        check_vma=False,
    )
```

profile of v0, /device:TPU:3, one launch (start us, length us, event | category | flops | bytes accessed | tf_op | source)
XLA Modules:
  0.0 282.3 jit_solution(15767832720702721144)
XLA Ops:
  0.0 3.8 %convert_element_type.31 = bf16[16,131072]{1,0:T(8,128)(2,1)S(1)} convert(s32[16,131072]{1,0:T(8,128)} %param.3) | non-fusion elementwise | flops 2097152 | bytes 12582912 | tf_op jit(solution)/shard_map/convert_element_type | solution.py:48
  3.8 0.0 copy-start.3
  3.8 0.0 copy-start.4
  3.8 2.3 copy.44
  6.1 0.3 slice.142
  6.5 0.6 copy.32
  7.0 3.8 %collective-permute-start = (bf16[16,15,2048]{2,0,1:T(8,128)(2,1)S(1)}, bf16[16,15,2048]{2,0,1:T(8,128)(2,1)S(1)}, u32[]{:S(2)}, u32[]{:S(2)}) collective-permute-start(bf16[16,15,2048]{2,0,1:T(8,128)(2,1)S(1)} %copy.32), channel_id=1, source_target_pairs={{0,1},{1,2},{2,3},{4,5},{5,6},{6,7},{8,9},{9,10},{10,11},{12,13},{... | collective-permute-start | bytes 2949128 | tf_op jit(solution)/shard_map/ppermute | solution.py:12
  10.8 0.0 copy-done.3
  10.8 0.1 fusion.33
  10.9 0.0 copy-done.4
  10.9 34.9 %sine_negate_fusion = (f32[1024,2048]{1,0:T(8,128)}, f32[1024,2048]{1,0:T(8,128)}) fusion(), kind=kLoop, calls=%fused_computation.48 | loop fusion | flops 31457280 | bytes 16777216 | tf_op jit(solution)/shard_map/neg | solution.py:20
  45.9 0.0 collective-permute-done
  45.9 0.5 copy.33
  46.4 1.8 convert_multiply_fusion
  48.2 16.8 %fusion.8 = bf16[16,64,2048]{2,1,0:T(8,128)(2,1)S(1)} fusion(f32[16,79,2048]{2,1,0:T(8,128)S(1)} %convert_multiply_fusion, f32[16]{0:T(128)S(1)} %convert_element_type.33, f32[2048]{0:T(1024)S(1)} %bitcast.65, f32[2048]{0:T(1024)S(1)} %bitcast.66, f32[2048]{0:T(1024)S(1)} %bitcast.52, f32[2048]{0:T(1024)S(1)} %bitcast.53, f32[2048]{0:T(1024)S(1)} %bitcast.54, ...), kind=kLoop, calls=%fused_computation.15 | loop fusion | flops 69206016 | bytes 138543168 | tf_op jit(solution)/shard_map/convert_element_type | solution.py:57
  65.0 0.0 copy-start.2
  65.0 1.9 copy-done.2
  67.0 15.2 %fusion.25 = f32[2048,1024]{1,0:T(8,128)} fusion(bf16[1024,2048]{1,0:T(8,128)(2,1)S(1)} %bitcast.49, f32[1024,2048]{1,0:T(8,128)} %get-tuple-element.23, f32[1024,2048]{1,0:T(8,128)} %get-tuple-element.24), kind=kOutput, calls=%fused_computation.51 | convolution fusion | flops 8610906112 | bytes 29360128 | tf_op jit(solution)/shard_map/dot_general | solution.py:63
  82.1 29.0 %multiply_convert_fusion = bf16[2048,1024]{1,0:T(8,128)(2,1)} fusion(f32[2048,1024]{1,0:T(8,128)} %fusion.25, bf16[1024,2048]{1,0:T(8,128)(2,1)} %bitcast.50, f32[1024,2048]{1,0:T(8,128)} %get-tuple-element.23, f32[1024,2048]{1,0:T(8,128)} %get-tuple-element.24), kind=kOutput, calls=%fused_computation.47 | convolution fusion | flops 8613003264 | bytes 33554432 | tf_op jit(solution)/shard_map/dot_general | solution.py:60
  111.1 11.5 %reshape.39 = bf16[2,1024,16,64]{3,2,1,0:T(8,128)(2,1)} reshape(bf16[2048,1024]{1,0:T(8,128)(2,1)} %multiply_convert_fusion) | data formatting | bytes 8388608 | tf_op jit(solution)/shard_map/reshape | solution.py:69
  122.7 8.1 %copy.46 = bf16[2,1024,16,64]{3,2,0,1:T(8,128)(2,1)} copy(bf16[2,1024,16,64]{3,2,1,0:T(8,128)(2,1)} %reshape.39) | data formatting | bytes 8388608 | tf_op jit(solution)/shard_map/reshape | solution.py:69
  130.7 14.3 %reshape.40 = bf16[128,2,8192]{2,1,0:T(2,128)(2,1)} reshape(bf16[1024,2,16,64]{3,2,1,0:T(8,128)(2,1)} %bitcast.44) | data formatting | bytes 8388608
  145.0 64.6 %all_to_all.15 = bf16[128,2,8192]{2,1,0:T(2,128)(2,1)} all-to-all(bf16[128,2,8192]{2,1,0:T(2,128)(2,1)} %reshape.40), channel_id=1, replica_groups=mesh['feed'=32,'tm'=4] {'feed','tm'}, dimensions={0} | all-to-all | bytes 8388608 | tf_op jit(solution)/shard_map/all_to_all | solution.py:71
  209.6 14.6 %reshape.41 = bf16[1024,2,16,64]{3,2,1,0:T(8,128)(2,1)} reshape(bf16[128,2,8192]{2,1,0:T(2,128)(2,1)} %all_to_all.15) | data formatting | bytes 8388608
  224.2 8.8 %copy.37 = bf16[2,8,128,16,64]{4,3,2,1,0:T(8,128)(2,1)} copy(bf16[2,8,128,16,64]{4,3,0,1,2:T(8,128)(2,1)} %bitcast.45) | data formatting | bytes 8388608 | tf_op jit(solution)/shard_map/all_to_all | solution.py:71
  233.0 5.9 %fusion.32 = (bf16[1,8,32,16,4,64]{5,3,4,2,1,0:T(8,128)(2,1)S(1)}, bf16[1,8,32,16,4,64]{5,3,4,2,1,0:T(8,128)(2,1)}) fusion(bf16[2,8,32,16,4,64]{5,3,4,2,1,0:T(8,128)(2,1)} %bitcast.43), kind=kLoop, calls=%fused_computation.56 | loop fusion | bytes 8388608 | tf_op jit(solution)/shard_map/slice | solution.py:76
  238.9 4.2 %copy.38 = bf16[1,8,32,16,4,64]{5,4,3,2,1,0:T(4,128)(2,1)} copy(bf16[1,8,32,16,4,64]{5,3,4,2,1,0:T(8,128)(2,1)S(1)} %get-tuple-element.5) | data formatting | bytes 4194304 | tf_op jit(solution)/shard_map/slice | solution.py:76
  243.1 6.0 %squeeze.6 = bf16[8,512,256]{2,1,0:T(8,128)(2,1)S(1)} reshape(bf16[1,8,32,16,4,64]{5,4,3,2,1,0:T(4,128)(2,1)} %copy.38) | data formatting | bytes 4194304 | tf_op jit(solution)/shard_map/squeeze | solution.py:76
  249.1 6.6 %copy.39 = bf16[1,8,32,16,4,64]{5,4,3,2,1,0:T(4,128)(2,1)} copy(bf16[1,8,32,16,4,64]{5,3,4,2,1,0:T(8,128)(2,1)} %get-tuple-element.6) | data formatting | bytes 4194304 | tf_op jit(solution)/shard_map/slice | solution.py:77
  255.7 7.0 %squeeze.7 = bf16[8,512,256]{2,1,0:T(8,128)(2,1)} reshape(bf16[1,8,32,16,4,64]{5,4,3,2,1,0:T(4,128)(2,1)} %copy.39) | data formatting | bytes 4194304 | tf_op jit(solution)/shard_map/squeeze | solution.py:77
  262.6 0.0 copy-start
  262.6 1.3 fusion.34
  263.9 0.3 copy-done
  264.2 1.3 fusion.35
  265.5 4.7 %subtract_bitcast_fusion = f32[8,1,512,512]{3,2,0,1:T(8,128)} fusion(f32[8,512,512]{2,1,0:T(8,128)S(1)} %fusion.35, bf16[8,512,256]{2,1,0:T(8,128)(2,1)S(1)} %squeeze.6, bf16[8,512,256]{2,1,0:T(8,128)(2,1)S(1)} %copy-done), kind=kOutput, calls=%fused_computation.45 | convolution fusion | flops 1075838976 | bytes 20971520 | tf_op jit(solution)/shard_map/dot_general | solution.py:28
  270.3 0.0 copy-start.1
  270.3 1.3 add_bitcast_fusion
  271.5 2.1 copy-done.1
  273.6 2.0 maximum_multiply_fusion
  275.7 6.4 %copy.40 = f32[8,2,512,512]{3,2,1,0:T(8,128)} copy(f32[8,2,512,512]{3,2,0,1:T(8,128)S(1)} %maximum_multiply_fusion) | data formatting | bytes 33554432 | tf_op jit(solution)/shard_map/div | solution.py:79
  (1 shorter events, 0.0 us)
Async XLA Ops:
  3.8 7.0 %copy-start.3 = (f32[16,2048]{1,0:T(8,128)S(1)}, f32[16,2048]{1,0:T(8,128)}, u32[]{:S(2)}) copy-start(f32[16,2048]{1,0:T(8,128)} %param.4) | copy-start | bytes 393220
  3.8 7.1 %copy-start.4 = (s32[16]{0:T(128)S(1)}, s32[16]{0:T(128)}, u32[]{:S(2)}) copy-start(s32[16]{0:T(128)} %param.5) | copy-start | bytes 196
  7.0 38.8 %collective-permute-start = (bf16[16,15,2048]{2,0,1:T(8,128)(2,1)S(1)}, bf16[16,15,2048]{2,0,1:T(8,128)(2,1)S(1)}, u32[]{:S(2)}, u32[]{:S(2)}) collective-permute-start(bf16[16,15,2048]{2,0,1:T(8,128)(2,1)S(1)} %copy.32), channel_id=1, source_target_pairs={{0,1},{1,2},{2,3},{4,5},{5,6},{6,7},{8,9},{9,10},{10,11},{12,13},{... | collective-permute-start | bytes 2949128 | tf_op jit(solution)/shard_map/ppermute | solution.py:12
  65.0 1.9 copy-start.2
  262.6 1.6 copy-start
  270.3 3.4 %copy-start.1 = (f32[8,1,512,512]{3,2,0,1:T(8,128)S(1)}, f32[8,1,512,512]{3,2,0,1:T(8,128)}, u32[]{:S(2)}) copy-start(f32[8,1,512,512]{3,2,0,1:T(8,128)} %subtract_bitcast_fusion) | copy-start | bytes 25165828
where the time goes:
time: 287 us; the launch traced here: 282 us
  local copies, waits for them, and re-layouts  101 us (35%)
  blocking collectives  64.6 us (23%)
  other arithmetic  59.4 us (21%)
  matrix products  52.7 us (18%)
  starting transfers between devices  3.77 us (1%)
    all_to_all x1, blocking collectives, per_device(): lax.all_to_all(spectra, ('feed', 'tm'), split_axis=1, concat_axis=2, tile...  64.6 us
    unnamed x13, local copies, waits for them, and re-layouts  35.5 us
    neg x1, other arithmetic, dft_tables(): -jnp.sin(phase_angle)  34.9 us
    dot_general x1, matrix products, per_device(): lax.dot_general(table_high, filtered, contract, preferred_element_type=jn...  29 us
    reshape x2, local copies, waits for them, and re-layouts, per_device(): spectra = (transformed / math.sqrt(frame_len)).astype(jnp.bfloat16).resha...  19.6 us
    convert_element_type x1, other arithmetic, per_device(): (running * kept_mask).astype(jnp.bfloat16)  16.8 us
    dot_general x1, matrix products, per_device(): lax.dot_general(table_low, filtered, contract, preferred_element_type=jnp...  15.2 us
    slice x2, local copies, waits for them, and re-layouts, per_device(): real_all = turned[0]  10.1 us
  transfers between devices with their start and end apart: 1, of which 0 were waited for; matrix products, arithmetic and copies ran while one was open for 12% of the time, Pallas kernels for 0%

commit v1 on v0

v1 whole, which is shorter than its diff:
```python
import functools
import math

import jax
import jax.numpy as jnp
import numpy as np
from jax import lax
from jax.experimental import pallas as pl
from jax.experimental.pallas import tpu as pltpu
from jax.sharding import PartitionSpec as P

LANES = 128
RADIX = 16


def coefficient_tables(frame_len):
    fine = frame_len // RADIX
    keep = fine // 2
    n2 = np.arange(fine)[None, :]
    k2 = np.arange(keep)[:, None]

    def wave(k1):
        phase = (k1 + RADIX * k2) * n2 % frame_len
        angle = phase * (2.0 * np.pi / frame_len)
        return np.cos(angle), np.sin(angle)

    zero = np.zeros((keep, fine))
    groups = []
    c0, s0 = wave(0)
    c8, s8 = wave(RADIX // 2)
    groups.append(np.block([[c0, zero], [-s0, zero], [zero, c8], [zero, -s8]]))
    for g in range(1, RADIX // 2):
        c, s = wave(g)
        d, t = wave(RADIX - g)
        groups.append(np.block([[c, s], [-s, c], [d, -t], [-t, -d]]))
    table = (np.stack(groups) / math.sqrt(frame_len)).astype(np.float32)
    high = table.astype(jnp.bfloat16)
    low = (table - high.astype(np.float32)).astype(jnp.bfloat16)
    return high, low


def real_dft16(x):
    R = np.float32(math.sqrt(0.5))
    C = np.float32(math.cos(math.pi / 8))
    S = np.float32(math.sin(math.pi / 8))
    s = [x[n] + x[n + 8] for n in range(8)]
    d = [x[n] - x[n + 8] for n in range(8)]
    a = [s[n] + s[n + 4] for n in range(4)]
    b = [s[n] - s[n + 4] for n in range(4)]
    out = {}
    a02, a13 = a[0] + a[2], a[1] + a[3]
    out[0] = a02 + a13
    out[8] = a02 - a13
    out[4] = (a[0] - a[2], a[3] - a[1])
    bm, bp = R * (b[1] - b[3]), R * (b[1] + b[3])
    out[2] = (b[0] + bm, -(b[2] + bp))
    out[6] = (b[0] - bm, b[2] - bp)
    e = [None] + [d[n] - d[8 - n] for n in (1, 2, 3)]
    f = [None] + [d[n] + d[8 - n] for n in (1, 2, 3)]
    re2, rf2 = R * e[2], R * f[2]
    p, q = d[0] + re2, d[0] - re2
    u, v = C * e[1] + S * e[3], S * e[1] - C * e[3]
    out[1] = p + u
    out[7] = p - u
    out[3] = q + v
    out[5] = q - v
    w, z = S * f[1] + C * f[3], C * f[1] - S * f[3]
    g, h = rf2 + d[4], rf2 - d[4]
    out[1] = (out[1], -(w + g))
    out[7] = (out[7], g - w)
    out[3] = (out[3], -(z + h))
    out[5] = (out[5], h - z)
    pairs = [(out[0], out[8])] + [out[k] for k in range(1, 8)]
    return pairs


def spectra_kernel(volt, halo, taps, gain, high, low, out, filt, yhi, ylo, spec):
    spec_dev, taps_count = 64, 16
    unroll = 16
    tiles = RADIX

    def pfb_block(n1, half, first):
        cols = lambda m: pl.ds(pl.multiple_of(m * 2048 + n1 * LANES, LANES), LANES)
        rows = slice(half * 8, half * 8 + 8)
        coeff = [
            jnp.broadcast_to(taps[p : p + 1, pl.ds(pl.multiple_of(n1 * LANES, LANES), LANES)], (8, LANES))
            for p in range(taps_count)
        ]
        scale = gain[rows, :]

        def run(m0, frame):
            acc = [None] * unroll
            for s in range(1 - taps_count, unroll):
                value = frame(s)
                for o in range(max(0, s), min(unroll, s + taps_count)):
                    term = coeff[o - s] * value
                    acc[o] = term if acc[o] is None else acc[o] + term
            for o in range(unroll):
                result = (acc[o] * scale).astype(jnp.bfloat16).astype(jnp.float32)
                filt[n1, pl.ds(half * spec_dev + m0 + o, 8, stride=2 * spec_dev), :] = result

        def first_frame(s):
            if s < 0:
                return halo[rows, cols(s + taps_count - 1)].astype(jnp.float32)
            return volt[rows, cols(s)].astype(jnp.float32)

        run(0, first_frame)

        def later(b, carry):
            run(b * unroll, lambda s: volt[rows, cols(b * unroll + s)].astype(jnp.float32))
            return carry

        lax.fori_loop(1, spec_dev // unroll, later, 0)

    def pfb_column(n1, carry):
        for half in range(2):
            pfb_block(n1, half, True)
        return carry

    lax.fori_loop(0, tiles, pfb_column, 0)

    def transform(r, carry):
        base = r * 256

        def coarse(b, inner):
            rows = pl.ds(pl.multiple_of(base + b * 16, 16), 16)
            to = pl.ds(pl.multiple_of(b * 16, 16), 16)
            pairs = real_dft16([filt[n1, rows, :] for n1 in range(RADIX)])
            for g, pair in enumerate(pairs):
                for half, value in enumerate(pair):
                    top = value.astype(jnp.bfloat16)
                    yhi[g, to, half * LANES : half * LANES + LANES] = top
                    ylo[g, to, half * LANES : half * LANES + LANES] = (
                        value - top.astype(jnp.float32)
                    ).astype(jnp.bfloat16)
            return inner

        lax.fori_loop(0, 16, coarse, 0)
        contract = (((1,), (1,)), ((), ()))

        def fine(g, inner):
            dot = functools.partial(
                lax.dot_general, dimension_numbers=contract, preferred_element_type=jnp.float32
            )
            value = dot(high[g], yhi[g]) + (dot(low[g], yhi[g]) + dot(high[g], ylo[g]))
            at = pl.multiple_of(g * 256, 256)
            spec[pl.ds(pl.multiple_of(2 * r * 2048 + at, 256), 256), :] = value[:, :LANES]
            spec[pl.ds(pl.multiple_of((2 * r + 1) * 2048 + at, 256), 256), :] = value[:, LANES:]
            return inner

        lax.fori_loop(0, 8, fine, 0)
        return carry

    lax.fori_loop(0, 4, transform, 0)
    left = lax.broadcasted_iota(jnp.int32, (8, LANES), 1) < 64

    def gather(k2, carry):
        for k1 in range(RADIX):
            h, c = divmod(k1, 8)
            if k1 == 8:
                g, q = 0, 1
            elif k1 > 8:
                g, q = RADIX - k1, 1
            else:
                g, q = k1, 0
            row = g * 256 + q * 128
            re = spec[pl.ds(row + k2, 8, stride=2048), :]
            im = spec[pl.ds(row + 64 + k2, 8, stride=2048), :]
            even = jnp.where(left, re, pltpu.roll(im, 64, 1))
            odd = jnp.where(left, pltpu.roll(re, 64, 1), im)
            out[2 * k2 + h, c] = jnp.concatenate([even, odd], axis=0).astype(jnp.bfloat16)
        return carry

    lax.fori_loop(0, 64, gather, 0)


def correlate_kernel(data, out):
    feeds = data.shape[0]
    parts = []
    turned = []
    for t in range(data.shape[1]):
        part = data[:, t, 0].reshape(feeds * 16, LANES)
        parts.append(part)
        wide = pltpu.roll(part.astype(jnp.float32), 64, 1)
        lane = lax.broadcasted_iota(jnp.int32, wide.shape, 1)
        turned.append(jnp.where(lane < 64, wide, -wide).astype(jnp.bfloat16))
    whole = jnp.concatenate(parts, axis=1)
    other = jnp.concatenate(turned, axis=1)
    contract = (((1,), (1,)), ((), ()))
    out[0, 0] = lax.dot_general(whole, whole, contract, preferred_element_type=jnp.float32) * (1.0 / 256)
    out[0, 1] = lax.dot_general(other, whole, contract, preferred_element_type=jnp.float32) * (1.0 / 256)


def per_device(voltages, pfb_taps, feed_flags):
    inputs_dev, samples_dev = voltages.shape
    taps_count, frame_len = pfb_taps.shape
    high, low = coefficient_tables(frame_len)
    rim = voltages[:, samples_dev - (taps_count - 1) * frame_len :].astype(jnp.bfloat16)
    halo = lax.ppermute(rim, "tm", [(i, i + 1) for i in range(lax.axis_size("tm") - 1)])
    gain = jnp.broadcast_to(feed_flags.astype(jnp.float32)[:, None] * (1.0 / 128), (inputs_dev, LANES))
    vmem = pl.BlockSpec(memory_space=pltpu.VMEM)
    spectra = pl.pallas_call(
        spectra_kernel,
        out_shape=jax.ShapeDtypeStruct((128, 8, 16, LANES), jnp.bfloat16),
        in_specs=[vmem] * 6,
        out_specs=vmem,
        scratch_shapes=[
            pltpu.VMEM((RADIX, 1024, LANES), jnp.float32),
            pltpu.VMEM((8, 256, 256), jnp.bfloat16),
            pltpu.VMEM((8, 256, 256), jnp.bfloat16),
            pltpu.VMEM((8 * 2048, LANES), jnp.float32),
        ],
        compiler_params=pltpu.CompilerParams(vmem_limit_bytes=60 * 2**20),
        name="spectra",
    )(voltages, halo, pfb_taps, gain, jnp.asarray(high), jnp.asarray(low))
    turned = lax.all_to_all(spectra, ("feed", "tm"), split_axis=0, concat_axis=0, tiled=True)
    turned = turned.reshape(32, 4, 8, 16, LANES)
    return pl.pallas_call(
        correlate_kernel,
        out_shape=jax.ShapeDtypeStruct((8, 2, 512, 512), jnp.float32),
        grid=(8,),
        in_specs=[pl.BlockSpec((32, 4, 1, 16, LANES), lambda c: (0, 0, c, 0, 0))],
        out_specs=pl.BlockSpec((1, 2, 512, 512), lambda c: (c, 0, 0, 0)),
        name="correlate",
    )(turned)


def solution(mesh):
    return jax.shard_map(
        per_device,
        mesh=mesh,
        in_specs=(P("feed", "tm"), P(), P("feed")),
        out_specs=P(("feed", "tm"), None, None, None),
        check_vma=False,
    )
```

time: 287 us -> 140 us (0.49); the launches traced: 282 us -> 140 us
  local copies, waits for them, and re-layouts: 101 us -> 0.96 us
  other arithmetic: 59.4 us -> 2.3 us
  Pallas kernels: 0 us -> 56.4 us
  matrix products: 52.7 us -> 0 us
  waiting for transfers between devices: 0.01 us -> 10.4 us
    pallas_call x0 -> x2, Pallas kernels: none -> 56.4 us  [the longest x1 45.2 us: per_device(): pl.pallas_call(spectra_kernel, out_shape=jax.ShapeDtypeStruct((128, 8, 16...]
    dot_general x6 -> x0, matrix products: 52.7 us -> none  [the longest x1 29 us: per_device(): lax.dot_general(table_high, filtered, contract, preferred_element_type=jn...]
    unnamed x13 -> x2, local copies, waits for them, and re-layouts: 35.5 us -> 0.21 us
    neg x1 -> x0, other arithmetic: 34.9 us -> none  [dft_tables(): -jnp.sin(phase_angle)]
    convert_element_type x3 -> x0, other arithmetic: 20.6 us -> none  [the longest x1 16.8 us: per_device(): (running * kept_mask).astype(jnp.bfloat16)]
    reshape x2 -> x0, local copies, waits for them, and re-layouts: 19.6 us -> none  [per_device(): spectra = (transformed / math.sqrt(frame_len)).astype(jnp.bfloat16).resha...]
    slice x6 -> x0, local copies, waits for them, and re-layouts: 17.7 us -> none  [the longest x2 10.1 us: per_device(): real_all = turned[0]]
    squeeze x2 -> x0, local copies, waits for them, and re-layouts: 12.9 us -> none  [the longest x1 6.95 us: per_device(): imag_all = turned[1]]
  transfers between devices with their start and end apart: 1 -> 1, of which waited for: 0 -> 1; matrix products, arithmetic and copies ran while one was open for 12% -> 0% of each run, Pallas kernels for 0% -> 0%
where the time goes in v1:
time: 140 us
  blocking collectives  65.9 us (47%)
  Pallas kernels  56.4 us (40%)
  waiting for transfers between devices  10.4 us (7%)
  starting transfers between devices  3.77 us (3%)
  other arithmetic  2.3 us (2%)
    all_to_all x1, blocking collectives, per_device(): lax.all_to_all(spectra, ('feed', 'tm'), split_axis=0, concat_axis=0, tile...  65.9 us
    pallas_call x1, Pallas kernels, per_device(): pl.pallas_call(spectra_kernel, out_shape=jax.ShapeDtypeStruct((128, 8, 16...  45.2 us
    pallas_call x1, Pallas kernels, per_device(): pl.pallas_call(correlate_kernel, out_shape=jax.ShapeDtypeStruct((8, 2, 51...  11.2 us
    ppermute x1, waiting for transfers between devices, per_device(): lax.ppermute(rim, 'tm', [(i, i + 1) for i in range(lax.axis_size('tm') -...  10.4 us
    ppermute x1, starting transfers between devices, per_device(): lax.ppermute(rim, 'tm', [(i, i + 1) for i in range(lax.axis_size('tm') -...  3.77 us
  transfers between devices with their start and end apart: 1, of which 1 were waited for; matrix products, arithmetic and copies ran while one was open for 0% of the time, Pallas kernels for 0%

profile of v1, /device:TPU:3, one launch (start us, length us, event | category | flops | bytes accessed | tf_op | source)
XLA Modules:
  0.0 139.7 jit_solution(15350358014331902243)
XLA Ops:
  0.0 1.6 %slice_convert_fusion = bf16[16,30720]{1,0:T(8,128)(2,1)S(1)} fusion(s32[16,131072]{1,0:T(8,128)} %volt.1), kind=kLoop, calls=%fused_computation | loop fusion | flops 491520 | bytes 2949120 | tf_op jit(solution)/shard_map/convert
  1.6 3.8 %collective-permute-start = (bf16[16,30720]{1,0:T(8,128)(2,1)S(1)}, bf16[16,30720]{1,0:T(8,128)(2,1)S(1)}, u32[]{:S(2)}, u32[]{:S(2)}) collective-permute-start(bf16[16,30720]{1,0:T(8,128)(2,1)S(1)} %slice_convert_fusion), channel_id=1, source_target_pairs={{0,1},{1,2},{2,3},{4,5},{5,6},{6,7},{8,9},{9,10},{10,11},{12,13},{... | collective-permute-start | bytes 2949128 | tf_op jit(solution)/shard_map/ppermute | solution.py:199
  5.4 0.7 convert_multiply_fusion
  6.1 10.4 %collective-permute-done.halo = bf16[16,30720]{1,0:T(8,128)(2,1)S(1)} collective-permute-done((bf16[16,30720]{1,0:T(8,128)(2,1)S(1)}, bf16[16,30720]{1,0:T(8,128)(2,1)S(1)}, u32[]{:S(2)}, u32[]{:S(2)}) %collective-permute-start) | collective-permute-done | bytes 983072 | tf_op jit(solution)/shard_map/ppermute | solution.py:199
  16.4 0.0 copy-start
  16.4 0.7 broadcast_in_dim.2.gain
  17.2 0.2 copy-done
  17.4 45.2 %spectra.1 = bf16[128,8,16,128]{3,2,1,0:T(8,128)(2,1)} custom-call(s32[16,131072]{1,0:T(8,128)} %volt.1, bf16[16,30720]{1,0:T(8,128)(2,1)} %copy-done, f32[16,2048]{1,0:T(8,128)} %taps.1, f32[16,128]{1,0:T(8,128)} %broadcast_in_dim.2.gain, bf16[8,256,256]{2,1,0:T(8,128)(2,1)} %constant.6.clone.high, bf16[8,256,256]{2,1,0:T(8,128)(2,1)} %constant.7.clone.low), custom_call_target="tpu_custom_call" | custom-call | tf_op jit(solution)/shard_map/spectra/pallas_call | solution.py:202
  62.6 65.9 %all_to_all.5 = bf16[128,8,16,128]{3,2,1,0:T(8,128)(2,1)} all-to-all(bf16[128,8,16,128]{3,2,1,0:T(8,128)(2,1)} %spectra.1), channel_id=1, replica_groups=mesh['feed'=32,'tm'=4] {'feed','tm'}, dimensions={0} | all-to-all | bytes 8388608 | tf_op jit(solution)/shard_map/all_to_all | solution.py:216
  128.5 11.2 %correlate.1 = f32[8,2,512,512]{3,2,1,0:T(8,128)} custom-call(bf16[32,4,8,16,128]{4,3,2,1,0:T(8,128)(2,1)} %bitcast.1), custom_call_target="tpu_custom_call" | custom-call | tf_op jit(solution)/shard_map/correlate/pallas_call | solution.py:218
Async XLA Ops:
  1.6 14.8 %collective-permute-start = (bf16[16,30720]{1,0:T(8,128)(2,1)S(1)}, bf16[16,30720]{1,0:T(8,128)(2,1)S(1)}, u32[]{:S(2)}, u32[]{:S(2)}) collective-permute-start(bf16[16,30720]{1,0:T(8,128)(2,1)S(1)} %slice_convert_fusion), channel_id=1, source_target_pairs={{0,1},{1,2},{2,3},{4,5},{5,6},{6,7},{8,9},{9,10},{10,11},{12,13},{... | collective-permute-start | bytes 2949128 | tf_op jit(solution)/shard_map/ppermute | solution.py:199
  16.4 1.0 copy-start
